TPU v7x, 256 devices: a whole 4x4x8 slice. The times are simulated.
256 devices in a mesh: row: 32 (over z, y), col: 8 (over x, core).
Axes of the slice: x: 4, y: 4, z: 8, core: 2. Of those that a mesh axis runs over, the one named last changes fastest.
Arguments:
- feat_a: bfloat16 [128, 1024, 128], P('row', 'col'), may hold values from -6 to 6
- feat_b: bfloat16 [32, 1024, 128], P('row', 'col'), may hold values from -6 to 6
- conv_weight: bfloat16 [3, 3, 128, 256], replicated, may hold values from -0.1875 to 0.1875
- conv_bias: float32 [256], replicated, may hold values from -3 to 3
- pair_lists: int32 [32, 2], replicated, may hold values from 0 to 7, as said below
- pair_counts: int32 [32], replicated, may hold values from 1 to 2, as said below
Outputs:
- log_conf_a: float32 [128, 1024], P('row', 'col')
- log_col_total: float32 [32, 1024], P('row', 'col')
Inputs may be any that keep to these rules, and one draw needn't show every extreme that they name: `pair_lists`: the first pair_counts[r] entries of row r are distinct B blocks; later entries repeat entry 0; every B block is listed by some A block. `pair_counts`: some A block lists 2 B blocks.
All inputs are finite; a program needn't handle non-finite values.
Results may differ from a plain program's by a relative error of at most 0.00037.
Values may be sent and summed in bfloat16 or wider, within the bound.
A program may use at most 64 MiB of HBM per device.

v0:
```python
import math

import jax
import jax.numpy as jnp
from jax import lax
from jax.sharding import PartitionSpec as P

KMAX = 2


def with_halo(cells, sides, width):
    for axis, dim in sides:
        count = lax.axis_size(axis)
        ends = count - 1
        head = lax.slice_in_dim(cells, 0, width, axis=dim)
        tail = lax.slice_in_dim(cells, cells.shape[dim] - width, cells.shape[dim], axis=dim)
        cells = jnp.concatenate(
            [
                lax.ppermute(tail, axis, [(i, (i + 1) % count) for i in range(ends)]),
                cells,
                lax.ppermute(head, axis, [((i + 1) % count, i) for i in range(ends)]),
            ],
            axis=dim,
        )
    return cells


def spread(value, axis, source):
    kept = jnp.where(lax.axis_index(axis) == source, value, 0).astype(value.dtype)
    return lax.psum(kept, axis)


def describe(padded, conv_weight, conv_bias):
    extent_y = padded.shape[0] - 2
    extent_x = padded.shape[1] - 2
    total = jnp.zeros((extent_y * extent_x, conv_weight.shape[3]), jnp.float32)
    for i in range(3):
        for j in range(3):
            window = padded[i : i + extent_y, j : j + extent_x].reshape(
                extent_y * extent_x, padded.shape[2]
            )
            total = total + jnp.dot(window, conv_weight[i, j], preferred_element_type=jnp.float32)
    total = total + conv_bias[None, :]
    unit = total * lax.rsqrt(jnp.mean(total * total, axis=1, keepdims=True) + 1e-06)
    return unit.astype(jnp.bfloat16)


def tile_totals(unit_a, block, piece_size, score_scale):
    pieces = block.reshape(-1, piece_size, block.shape[1])

    def accumulate(row_sum, piece):
        weights = jnp.exp(
            jnp.einsum("nd,md->nm", unit_a, piece, preferred_element_type=jnp.float32) * score_scale
        )
        return (row_sum + jnp.sum(weights, axis=1), jnp.sum(weights, axis=0))

    row_sum, col_parts = lax.scan(accumulate, jnp.zeros((unit_a.shape[0],), jnp.float32), pieces)
    return (row_sum, col_parts.reshape(-1))


def tile_best(unit_a, block, logs, piece_size, score_scale):
    pieces = block.reshape(-1, piece_size, block.shape[1])
    log_pieces = logs.reshape(-1, piece_size)

    def accumulate(running, inputs):
        piece, log_piece = inputs
        scored = (
            jnp.einsum("nd,md->nm", unit_a, piece, preferred_element_type=jnp.float32) * score_scale
        )
        candidate = jnp.max(2.0 * scored - log_piece[None, :], axis=1)
        return (jnp.maximum(running, candidate), None)

    start = jnp.full((unit_a.shape[0],), -jnp.inf, jnp.float32)
    running, unused = lax.scan(accumulate, start, (pieces, log_pieces))
    return running


def local(feat_a, feat_b, conv_weight, conv_bias, pair_lists, pair_counts):
    padded_a = with_halo(feat_a, (("row", 0), ("col", 1)), 1)
    padded_b = with_halo(feat_b, (("row", 0), ("col", 1)), 1)
    unit_a = describe(padded_a, conv_weight, conv_bias)
    desc_width = conv_weight.shape[3]
    unit_b = describe(padded_b, conv_weight, conv_bias).reshape(
        feat_b.shape[0], feat_b.shape[1], desc_width
    )
    row_index = lax.axis_index("row")
    col_index = lax.axis_index("col")
    listed = lax.dynamic_index_in_dim(pair_lists, row_index, 0, keepdims=False)
    live_count = lax.dynamic_index_in_dim(pair_counts, row_index, 0, keepdims=False)
    own_block = lax.all_gather(unit_b, "row", axis=0, tiled=True)
    blocks = []
    for k in range(KMAX):
        fetched = spread(own_block, "col", listed[k])
        blocks.append(fetched.reshape(-1, desc_width))
    block_cells = blocks[0].shape[0]
    piece_size = math.gcd(block_cells, 1024)
    score_scale = 1.0 / (desc_width * 0.1)
    n_blocks = lax.axis_size("col")
    cells_a = unit_a.shape[0]
    row_tot = jnp.zeros((cells_a,), jnp.float32)
    col_tot = jnp.zeros((n_blocks, block_cells), jnp.float32)
    for k in range(KMAX):
        block = blocks[k]
        row_part, col_part = lax.cond(
            k < live_count,
            lambda: tile_totals(unit_a, block, piece_size, score_scale),
            lambda: (jnp.zeros((cells_a,), jnp.float32), jnp.zeros((block_cells,), jnp.float32)),
        )
        row_tot = row_tot + row_part
        current = lax.dynamic_index_in_dim(col_tot, listed[k], 0, keepdims=False)
        col_tot = lax.dynamic_update_index_in_dim(col_tot, current + col_part, listed[k], 0)
    col_all = lax.psum(col_tot, ("row", "col"))
    log_col = jnp.log(col_all)
    running = jnp.full((cells_a,), -jnp.inf, jnp.float32)
    for k in range(KMAX):
        block = blocks[k]
        logs = lax.dynamic_index_in_dim(log_col, listed[k], 0, keepdims=False)
        running = lax.cond(
            k < live_count,
            lambda: jnp.maximum(running, tile_best(unit_a, block, logs, piece_size, score_scale)),
            lambda: running,
        )
    log_conf_a = (running - jnp.log(row_tot)).reshape(feat_a.shape[0], feat_a.shape[1])
    own_cells = feat_b.shape[0] * feat_b.shape[1]
    own_logs = lax.dynamic_slice(log_col, (col_index, row_index * own_cells), (1, own_cells))
    return (log_conf_a, own_logs)


def solution(mesh):
    in_specs = (P("row", "col", None), P("row", "col", None), P(), P(), P(), P())
    out_specs = (P("row", "col"), P("row", "col"))
    return jax.shard_map(local, mesh=mesh, in_specs=in_specs, out_specs=out_specs, check_vma=False)
```

profile of v0, /device:TPU:1, one launch (start us, length us, event | category | flops | bytes accessed | tf_op | source)
XLA Modules:
  0.0 476.9 jit_solution(670848616781209058)
XLA Ops:
  7.3 4.2 collective-permute-start
  11.4 1.3 collective-permute-start.1
  12.7 1.0 fusion.46
  13.8 0.8 constant_dynamic-update-slice_fusion.1
  14.5 1.8 collective-permute-done.1
  16.3 4.0 collective-permute-start.3
  20.4 3.0 collective-permute-start.2
  23.4 1.0 fusion.38
  24.4 1.0 fusion.56
  25.4 1.0 fusion.41
  26.4 1.0 fusion.49
  27.4 1.0 fusion.34
  28.3 1.0 fusion.52
  29.8 0.7 multiply_convert_fusion.1
  30.6 3.2 collective-permute-start.4
  33.8 1.3 collective-permute-start.5
  35.2 0.6 fusion.104
  39.6 0.6 dynamic_slice.57
  42.9 3.2 collective-permute-start.6
  46.0 1.9 collective-permute-start.7
  48.5 2.8 collective-permute-done.7
  51.5 57.2 %all-gather.3.cloned.1.call-done = bf16[4096,256]{1,0:T(8,128)(2,1)} async-done(((bf16[128,256]{1,0:T(8,128)(2,1)}), bf16[4096,256]{1,0:T(8,128)(2,1)}) %all-gather.3.cloned.1.call-update) | async-done | bytes 2097168 | tf_op jit(solution)/shard_map/all_gather | solution.py:90
  108.7 3.8 broadcast_select_fusion
  114.7 75.2 %all-reduce.6.cloned.1.call-done = (bf16[32,128,256]{2,1,0:T(8,128)(2,1)}, bf16[32,128,256]{2,1,0:T(8,128)(2,1)}) async-done(((bf16[32,128,256]{2,1,0:T(8,128)(2,1)}, bf16[32,128,256]{2,1,0:T(8,128)(2,1)}), (bf16[32,128,256]{2,1,0:T(8,128)(2,1)}, bf16[32,128,256]{2,1,0:T(8,128)(2,1)})) %all-reduce.6.cloned.1.call-update) | async-done | bytes 4194320 | tf_op jit(solution)/shard_map/psum | solution.py:30
  189.9 11.7 %conditional.4 = (f32[512]{0:T(512)}, f32[1,4096]{1,0:T(1,128)S(1)}) conditional(s32[]{:T(128)} %bitcast.5, () %tuple.76, (bf16[32,128,256]{2,1,0:T(8,128)(2,1)}, bf16[512,256]{0,1:T(8,128)(2,1)S(1)}) %tuple.77), branch_computations={%region_3.4_spmd, %region_4.9_spmd} | conditional | flops 270007808 | bytes 1364151 | solution.py:104
  190.0 11.5 %while.51 = (s32[]{:T(128)}, f32[512]{0:T(512)}, f32[4,1024]{1,0:T(4,128)S(1)}, bf16[4,1024,256]{2,1,0:T(8,128)(2,1)}, bf16[512,256]{1,0:T(8,128)(2,1)S(1)}, /*index=5*/s32[]{:T(128)}, s32[]{:T(128)}) while((s32[]{:T(128)}, f32[512]{0:T(512)}, f32[4,1024]{1,0:T(4,128)S(1)}, bf16[4,1024,256]{2,1,0:T(8,128)(2,1)}, ...), condition=%wide.region_8.8_spmd.clone, body=%wide.region_5.7_spmd.clone.sunk | while | flops 270007808 | bytes 807015 | solution.py:57
  190.0 1.8 fusion.133
  191.8 0.6 select_add_fusion.5
  192.5 1.7 fusion.133
  194.2 1.3 select_add_fusion.5
  195.5 1.7 fusion.133
  197.2 1.3 select_add_fusion.5
  198.5 1.7 fusion.133
  200.2 1.3 select_add_fusion.5
  202.0 7.3 %conditional.5 = (f32[512]{0:T(512)}, f32[4096]{0:T(1024)S(1)}) conditional(s32[]{:T(128)} %bitcast.4, () %tuple.78, (bf16[32,128,256]{2,1,0:T(8,128)(2,1)S(1)}, bf16[512,256]{0,1:T(8,128)(2,1)S(1)}) %tuple.186), branch_computations={%region_10.11_spmd, %region_11.16_spmd} | conditional | flops 270007808 | bytes 1364151 | solution.py:104
  202.2 7.1 %while.52 = (s32[]{:T(128)}, f32[512]{0:T(512)}, f32[4,1024]{1,0:T(4,128)S(1)}, bf16[4,1024,256]{2,1,0:T(8,128)(2,1)S(1)}, bf16[512,256]{1,0:T(8,128)(2,1)S(1)}, /*index=5*/s32[]{:T(128)}, s32[]{:T(128)}) while((s32[]{:T(128)}, f32[512]{0:T(512)}, f32[4,1024]{1,0:T(4,128)S(1)}, bf16[4,1024,256]{2,1,0:T(8,128)(2,1)S(1)}, ...), condition=%wide.region_15.15_spmd.clone, body=%wide.region_12.14_spmd.clone.sunk | while | flops 270007808 | bytes 807015 | solution.py:57
  202.2 0.6 fusion.131
  202.8 0.6 select_add_fusion.4
  203.5 0.6 fusion.131
  204.1 1.2 select_add_fusion.4
  205.4 0.6 fusion.131
  206.1 1.2 select_add_fusion.4
  207.4 0.6 fusion.131
  208.0 1.2 select_add_fusion.4
  209.8 0.6 copy-done.3
  210.4 242.6 %all-reduce.4.cloned.1.call-done = f32[8,4096]{1,0:T(8,128)} async-done(((f32[8,4096]{1,0:T(8,128)}), f32[8,4096]{1,0:T(8,128)}) %all-reduce.4.cloned.1.call-update) | async-done | bytes 131088 | tf_op jit(solution)/shard_map/psum | solution.py:112
  453.1 0.9 log.6
  454.0 10.9 %conditional.6 = (f32[512]{0:T(512)}) conditional(s32[]{:T(128)} %bitcast.5, () %tuple.75, (bf16[32,128,256]{2,1,0:T(8,128)(2,1)}, f32[8,4096]{1,0:T(8,128)S(1)}, bf16[512,256]{0,1:T(8,128)(2,1)S(1)}, s32[]{:T(128)}) %tuple.104), branch_computations={%region_17.18_spmd, %region_18.22_spmd.clone} | conditional | flops 270008832 | bytes 1396915 | solution.py:118
  454.2 10.7 %while.53 = (s32[]{:T(128)}, f32[512]{0:T(512)}, bf16[4,1024,256]{2,1,0:T(8,128)(2,1)}, bf16[512,256]{1,0:T(8,128)(2,1)S(1)}, f32[4,1024]{1,0:T(4,128)S(1)}, /*index=5*/s32[]{:T(128)}, s32[]{:T(128)}) while((s32[]{:T(128)}, f32[512]{0:T(512)}, bf16[4,1024,256]{2,1,0:T(8,128)(2,1)}, bf16[512,256]{1,0:T(8,128)(2,1)S(1)}, ...), condition=%wide.region_21.21_spmd.clone, body=%wide.region_19.20_spmd.clone.sunk | while | flops 270008832 | bytes 807015 | solution.py:74
  454.3 1.5 subtract_reduce_fusion.5
  455.8 0.6 select_maximum_fusion.5
  456.4 1.5 subtract_reduce_fusion.5
  457.9 1.3 select_maximum_fusion.5
  459.2 1.5 subtract_reduce_fusion.5
  460.8 1.3 select_maximum_fusion.5
  462.1 1.5 subtract_reduce_fusion.5
  463.6 1.3 select_maximum_fusion.5
  464.9 3.6 conditional.7
  465.1 2.1 while.54
  465.7 0.5 subtract_reduce_fusion.4
  466.7 0.5 subtract_reduce_fusion.4
  467.3 1.3 max.15
  468.5 0.6 dynamic_slice.61
  469.1 1.3 subtract_bitcast_fusion
  (92 shorter events, 6.4 us)
Async XLA Ops:
  7.2 28.0 %copy-start = (s32[32,2]{0,1:T(2,128)S(1)}, s32[32,2]{0,1:T(2,128)}, u32[]{:S(2)}) copy-start(s32[32,2]{0,1:T(2,128)} %param.26) | copy-start | bytes 772
  7.2 22.2 %copy-start.1 = (bf16[3,3,128,256]{3,2,1,0:T(8,128)(2,1)S(1)}, bf16[3,3,128,256]{3,2,1,0:T(8,128)(2,1)}, u32[]{:S(2)}) copy-start(bf16[3,3,128,256]{3,2,1,0:T(8,128)(2,1)} %param.24) | copy-start | bytes 1769476
  7.2 22.3 %copy-start.4 = (f32[256]{0:T(256)S(1)}, f32[256]{0:T(256)}, u32[]{:S(2)}) copy-start(f32[256]{0:T(256)} %param.25) | copy-start | bytes 3076
  7.2 23.4 %copy-start.2 = (bf16[4,128,128]{2,1,0:T(8,128)(2,1)S(1)}, bf16[4,128,128]{2,1,0:T(8,128)(2,1)}, u32[]{:S(2)}) copy-start(bf16[4,128,128]{2,1,0:T(8,128)(2,1)} %param.22) | copy-start | bytes 393220
  7.2 32.4 %copy-start.6 = (s32[32]{0:T(128)S(1)}, s32[32]{0:T(128)}, u32[]{:S(2)}) copy-start(s32[32]{0:T(128)} %param.27) | copy-start | bytes 388
  7.2 101.5 %all-gather.3.cloned.1.call-start = ((), (), s32[]{:S(2)}) async-start(), calls=%async_computation.1 | async-start | bytes 2162688 | tf_op jit(solution)/shard_map/all_gather | solution.py:90
  7.3 6.5 %collective-permute-start = (bf16[1,128,128]{2,1,0:T(8,128)(2,1)}, bf16[1,128,128]{2,1,0:T(8,128)(2,1)S(1)}, u32[]{:S(2)}, u32[]{:S(2)}) collective-permute-start(bf16[1,128,128]{2,1,0:T(8,128)(2,1)} %param.23), channel_id=1, source_target_pairs={{0,8},{8,16},{16,24},{24,32},{32,40},{40,48},{48,56},{56,64},{64,7... | collective-permute-start | bytes 98312 | tf_op jit(solution)/shard_map/ppermute | solution.py:19
  11.4 4.9 %collective-permute-start.1 = (bf16[1,128,128]{2,1,0:T(8,128)(2,1)}, bf16[1,128,128]{2,1,0:T(8,128)(2,1)S(1)}, u32[]{:S(2)}, u32[]{:S(2)}) collective-permute-start(bf16[1,128,128]{2,1,0:T(8,128)(2,1)} %param.23), channel_id=1, source_target_pairs={{8,0},{16,8},{24,16},{32,24},{40,32},{48,40},{56,48},{64,56},{72,6... | collective-permute-start | bytes 98312 | tf_op jit(solution)/shard_map/ppermute | solution.py:21
  16.3 11.0 %collective-permute-start.3 = (bf16[3,1,128]{2,1,0:T(2,128)(2,1)S(1)}, bf16[3,1,128]{2,1,0:T(2,128)(2,1)S(1)}, u32[]{:S(2)}, u32[]{:S(2)}) collective-permute-start(bf16[3,1,128]{2,1,0:T(2,128)(2,1)S(1)} %get-tuple-element.423), channel_id=1, source_target_pairs={{1,0},{2,1},{3,2},{4,3},{5,4},{6,5},{7,6},{9,8},{10,9},{11,10},{12... | collective-permute-start | bytes 2312 | tf_op jit(solution)/shard_map/ppermute | solution.py:21
  20.4 5.0 %collective-permute-start.2 = (bf16[3,1,128]{2,1,0:T(2,128)(2,1)S(1)}, bf16[3,1,128]{2,1,0:T(2,128)(2,1)S(1)}, u32[]{:S(2)}, u32[]{:S(2)}) collective-permute-start(bf16[3,1,128]{2,1,0:T(2,128)(2,1)S(1)} %get-tuple-element.422), channel_id=1, source_target_pairs={{0,1},{1,2},{2,3},{3,4},{4,5},{5,6},{6,7},{8,9},{9,10},{10,11},{11... | collective-permute-start | bytes 2312 | tf_op jit(solution)/shard_map/ppermute | solution.py:19
  30.5 159.3 %all-reduce.6.cloned.1.call-start = ((), (), s32[]{:S(2)}) async-start(), calls=%async_computation.2 | async-start | bytes 8388608 | tf_op jit(solution)/shard_map/psum | solution.py:30
  30.6 12.1 %collective-permute-start.4 = (bf16[1,128,128]{2,1,0:T(8,128)(2,1)S(1)}, bf16[1,128,128]{2,1,0:T(8,128)(2,1)S(1)}, u32[]{:S(2)}, u32[]{:S(2)}) collective-permute-start(bf16[1,128,128]{2,1,0:T(8,128)(2,1)S(1)} %get-tuple-element.421), channel_id=1, source_target_pairs={{0,8},{8,16},{16,24},{24,32},{32,40},{40,48},{48,56},{56,64},{64,7... | collective-permute-start | bytes 98312 | tf_op jit(solution)/shard_map/ppermute | solution.py:19
  33.8 8.9 %collective-permute-start.5 = (bf16[1,128,128]{2,1,0:T(8,128)(2,1)S(1)}, bf16[1,128,128]{2,1,0:T(8,128)(2,1)S(1)}, u32[]{:S(2)}, u32[]{:S(2)}) collective-permute-start(bf16[1,128,128]{2,1,0:T(8,128)(2,1)S(1)} %get-tuple-element.420), channel_id=1, source_target_pairs={{8,0},{16,8},{24,16},{32,24},{40,32},{48,40},{56,48},{64,56},{72,6... | collective-permute-start | bytes 98312 | tf_op jit(solution)/shard_map/ppermute | solution.py:21
  42.9 5.6 %collective-permute-start.6 = (bf16[6,1,128]{2,1,0:T(2,128)(2,1)S(1)}, bf16[6,1,128]{2,1,0:T(2,128)(2,1)S(1)}, u32[]{:S(2)}, u32[]{:S(2)}) collective-permute-start(bf16[6,1,128]{2,1,0:T(2,128)(2,1)S(1)} %get-tuple-element.415), channel_id=1, source_target_pairs={{0,1},{1,2},{2,3},{3,4},{4,5},{5,6},{6,7},{8,9},{9,10},{10,11},{11... | collective-permute-start | bytes 4616 | tf_op jit(solution)/shard_map/ppermute | solution.py:19
  46.0 5.3 %collective-permute-start.7 = (bf16[6,1,128]{2,1,0:T(2,128)(2,1)S(1)}, bf16[6,1,128]{2,1,0:T(2,128)(2,1)S(1)}, u32[]{:S(2)}, u32[]{:S(2)}) collective-permute-start(bf16[6,1,128]{2,1,0:T(2,128)(2,1)S(1)} %get-tuple-element.416), channel_id=1, source_target_pairs={{1,0},{2,1},{3,2},{4,3},{5,4},{6,5},{7,6},{9,8},{10,9},{11,10},{12... | collective-permute-start | bytes 4616 | tf_op jit(solution)/shard_map/ppermute | solution.py:21
  112.6 340.5 %all-reduce.4.cloned.1.call-start = ((), (), s32[]{:S(2)}) async-start(), calls=%async_computation | async-start | bytes 262144 | tf_op jit(solution)/shard_map/psum | solution.py:112
  189.9 12.2 %copy-start.5 = (bf16[32,128,256]{2,1,0:T(8,128)(2,1)S(1)}, bf16[32,128,256]{2,1,0:T(8,128)(2,1)}, u32[]{:S(2)}) copy-start(bf16[32,128,256]{2,1,0:T(8,128)(2,1)} %get-tuple-element.403) | copy-start | bytes 6291460
  209.7 0.6 copy-start.3
Sparse Core Ops, SparseCore 0:
  30.7 78.0 all-gather.2
  112.7 77.0 all-reduce.5
  210.5 242.4 all-reduce.3
where the time goes:
time: 479 us; the launch traced here: 477 us
  waiting for transfers between devices  380 us (79%)
  matrix products  27 us (6%)
  starting transfers between devices  22.2 us (5%)
  other arithmetic  20.7 us (4%)
  between operations  20.5 us (4%)
  local copies, waits for them, and re-layouts  6.21 us (1%)
    psum x1, waiting for transfers between devices, local(): col_all = lax.psum(col_tot, ('row', 'col'))  243 us
    psum x1, waiting for transfers between devices, spread(): return lax.psum(kept, axis)  75.2 us
    all_gather x1, waiting for transfers between devices, local(): own_block = lax.all_gather(unit_b, 'row', axis=0, tiled=True)  57.2 us
    dot_general x16, matrix products, accumulate(): jnp.einsum('nd,md->nm', unit_a, piece, preferred_element_type=jnp.float32)  17.3 us
    ppermute x4, starting transfers between devices, with_halo(): lax.ppermute(tail, axis, [(i, (i + 1) % count) for i in range(ends)])  13.6 us
    dot_general x18, matrix products, describe(): jnp.dot(window, conv_weight[i, j], preferred_element_type=jnp.float32)  9.76 us
  transfers between devices with their start and end apart: 11, of which 5 were waited for; matrix products, arithmetic and copies ran while one was open for 2% of the time, Pallas kernels for 0%

commit v1 on v0

v1 whole, which is shorter than its diff:
```python
import functools
import math

import jax
import jax.numpy as jnp
from jax import lax
from jax.experimental import pallas as pl
from jax.experimental.pallas import tpu as pltpu
from jax.sharding import PartitionSpec as P

KMAX = 2
NY = 4
STRIP = 16
MESH = pl.DeviceIdType.MESH
F32 = jnp.float32
BF16 = jnp.bfloat16


def remote(src, dst, send_sem, recv_sem, row, col):
    return pltpu.make_async_remote_copy(
        src_ref=src,
        dst_ref=dst,
        send_sem=send_sem,
        recv_sem=recv_sem,
        device_id=(row, col),
        device_id_type=MESH,
    )


def taps(center, left, right):
    rows, cols, ch = center.shape
    flat = center.reshape(rows * cols, ch)
    place = lax.broadcasted_iota(jnp.int32, center.shape, 1)
    before = pltpu.roll(flat, 1, 0).reshape(center.shape)
    after = pltpu.roll(flat, rows * cols - 1, 0).reshape(center.shape)
    before = jnp.where(place == 0, left, before)
    after = jnp.where(place == cols - 1, right, after)
    return jnp.concatenate(
        [before.astype(BF16), center.astype(BF16), after.astype(BF16)], axis=2
    )


def normalized(total, bias):
    total = total + bias
    mean = jnp.mean(total * total, axis=1, keepdims=True)
    return (total * lax.rsqrt(mean + 1e-06)).astype(BF16)


def kernel(
    n_row, n_col, scale,
    feat_a, feat_b, weight, bias, lists, counts,
    conf_out, logs_out,
    hrow, hcol, brow, unit, ball, taps_a, taps_b, desc_a, desc_b,
    scores, colacc, coly, colz, lchunk, lrecv, logfull,
    rowpart, rowrecv, maxpart, maxrecv,
    halo_s, halo_r, bx_s, bx_r, bz_s, bz_r, by_s, by_r,
    ax_s, ax_r, ap_s, ap_r, cy_s, cy_r, cz_s, cz_r,
    rs_s, rs_r, lg_s, lg_r, mx_s, mx_r,
):
    r = lax.axis_index("row")
    c = lax.axis_index("col")
    nz = n_row // NY
    nx = n_col // 2
    z = r // NY
    y = r % NY
    x = c // 2
    core = c % 2
    up = (r + n_row - 1) % n_row
    down = (r + 1) % n_row
    lf = (c + n_col - 1) % n_col
    rt = (c + 1) % n_col

    def zrow(step):
        return ((z + step) % nz) * NY + y

    def yrow(step):
        return z * NY + (y + step) % NY

    barrier = pltpu.get_barrier_semaphore()
    partners = [(r, (c + s) % n_col) for s in range(1, n_col)]
    partners += [(yrow(s), c) for s in range(1, NY)]
    partners += [(zrow(s), c) for s in range(1, nz)]
    partners += [(v, h) for v in (up, down) for h in (lf, c, rt)]
    for device in partners:
        pl.semaphore_signal(barrier, inc=1, device_id=device, device_id_type=MESH)
    pl.semaphore_wait(barrier, len(partners))

    sends = []

    def go(copy):
        copy.start()
        sends.append(copy)
        return copy

    bx = []
    for s in range(1, n_col):
        bx.append(
            go(remote(feat_b, brow.at[c], bx_s.at[s], bx_r.at[c], r, (c + s) % n_col))
        )
    last = feat_a.shape[1] - STRIP
    edges = [
        (feat_a.at[3], hrow.at[0], down, c),
        (feat_a.at[0], hrow.at[1], up, c),
        (feat_a.at[:, pl.ds(last, STRIP)], hcol.at[0, pl.ds(1, 4)], r, rt),
        (feat_a.at[:, pl.ds(0, STRIP)], hcol.at[1, pl.ds(1, 4)], r, lf),
        (feat_a.at[3, pl.ds(last, STRIP)], hcol.at[0, 0], down, rt),
        (feat_a.at[3, pl.ds(0, STRIP)], hcol.at[1, 0], down, lf),
        (feat_a.at[0, pl.ds(last, STRIP)], hcol.at[0, 5], up, rt),
        (feat_a.at[0, pl.ds(0, STRIP)], hcol.at[1, 5], up, lf),
    ]
    halos = [
        go(remote(src, dst, halo_s.at[i], halo_r.at[i], row, col))
        for i, (src, dst, row, col) in enumerate(edges)
    ]

    brow[c] = feat_b[...]
    for s in range(1, n_col):
        src = (c + n_col - s) % n_col
        remote(feat_b, brow.at[src], bx_s.at[s], bx_r.at[src], r, src).wait_recv()

    strip = pl.ds(pl.multiple_of(c * STRIP, STRIP), STRIP)
    width = feat_b.shape[0]
    unit[pl.ds(0, n_col)] = brow[:, strip, :]
    entry = lax.broadcasted_iota(jnp.int32, (2 * n_col, n_col * width), 0)
    column = lax.broadcasted_iota(jnp.int32, (2 * n_col, n_col * width), 1)
    wanted = jnp.where(
        entry < n_col,
        entry * width + c * STRIP - 1,
        (entry - n_col) * width + c * STRIP + STRIP,
    )
    pick = jnp.where(column == wanted, 1.0, 0.0).astype(BF16)
    row_all = brow[...].reshape(n_col * width, brow.shape[2])
    unit[n_col] = jnp.dot(pick, row_all, preferred_element_type=F32).astype(BF16)

    zs = [4, 3, 5, 2, 6, 1, 7]
    for s in zs:
        go(remote(unit, ball.at[r], bz_s.at[s], bz_r.at[z], zrow(s), c))
    for s in range(1, NY):
        go(remote(unit, ball.at[r], by_s.at[0, s], by_r.at[z, y], yrow(s), c))
    ball[r] = unit[...]

    for i, (src, dst, row, col) in enumerate(edges):
        halos[i].wait_recv()
    zero = jnp.zeros((), F32)
    top = jnp.where(r == 0, zero, hrow[0].astype(F32))
    bottom = jnp.where(r == n_row - 1, zero, hrow[1].astype(F32))
    center = jnp.concatenate([top[None], feat_a[...].astype(F32), bottom[None]], axis=0)
    sixth = lax.broadcasted_iota(jnp.int32, (6, 1, hcol.shape[3]), 0)
    outside = ((sixth == 0) & (r == 0)) | ((sixth == 5) & (r == n_row - 1))
    left = jnp.where(outside | (c == 0), zero, hcol[0].astype(F32)[:, STRIP - 1 : STRIP])
    right = jnp.where(outside | (c == n_col - 1), zero, hcol[1].astype(F32)[:, 0:1])
    taps_a[...] = taps(center, left, right)
    n_a = 4 * feat_a.shape[1]
    total = jnp.zeros((n_a, desc_a.shape[2]), F32)
    for i in range(3):
        window = taps_a[pl.ds(i, 4)].reshape(n_a, taps_a.shape[2])
        total = total + jnp.dot(window, weight[i], preferred_element_type=F32)
    desc_a[c] = normalized(total, bias[...])
    mate = x * 2 + (1 - core)
    for s in (2, 1, 3):
        far = ((x + s) % nx) * 2 + core
        go(remote(desc_a.at[c], desc_a.at[c], ax_s.at[s], ax_r.at[x], r, far))
    go(remote(desc_a.at[c], desc_a.at[c], ap_s.at[0], ap_r.at[x], r, mate))

    for i, s in enumerate((1, 7, 2, 6, 3, 5, 4)):
        src_z = (z + s) % nz
        slot = ball.at[src_z * NY + y]
        remote(unit, slot, bz_s.at[s], bz_r.at[src_z], r, c).wait_recv()
        for t in range(1, NY):
            go(remote(slot, slot, by_s.at[i + 1, t], by_r.at[src_z, y], yrow(t), c))
    for s in (1, 3, 2):
        src_x = (x + s) % nx
        slot = desc_a.at[src_x * 2 + core]
        remote(slot, slot, ax_s.at[s], ax_r.at[src_x], r, c).wait_recv()
        go(remote(slot, slot, ap_s.at[s], ap_r.at[src_x], r, mate))
    for s in (0, 1, 7, 2, 6, 3, 5, 4):
        src_z = (z + s) % nz
        for t in range(1, NY):
            src_y = (y + t) % NY
            slot = ball.at[src_z * NY + src_y]
            remote(slot, slot, by_s.at[0, t], by_r.at[src_z, src_y], r, c).wait_recv()

    listed = [lists[r, k] for k in range(KMAX)]
    live = [counts[r] > k for k in range(KMAX)]
    n_h = n_row
    n_b = n_h * STRIP
    taps_b[0] = jnp.zeros(taps_b.shape[1:], BF16)
    taps_b[n_h + 1] = jnp.zeros(taps_b.shape[1:], BF16)
    beside = ball[:, n_col].astype(F32)
    entry = lax.broadcasted_iota(jnp.int32, beside.shape, 1)
    for k in range(KMAX):
        block = ball[:, listed[k]].astype(F32)
        left = jnp.sum(jnp.where(entry == listed[k], beside, 0.0), axis=1, keepdims=True)
        right = jnp.sum(
            jnp.where(entry == listed[k] + n_col, beside, 0.0), axis=1, keepdims=True
        )
        taps_b[pl.ds(1, n_h)] = taps(block, left, right)
        total = jnp.zeros((n_b, desc_b.shape[2]), F32)
        for i in range(3):
            window = taps_b[pl.ds(i, n_h)].reshape(n_b, taps_b.shape[2])
            total = total + jnp.dot(window, weight[i], preferred_element_type=F32)
        desc_b[k] = normalized(total, bias[...])

    for s in range(nx):
        src_x = (x + s) % nx
        slot = desc_a.at[src_x * 2 + (1 - core)]
        remote(slot, slot, ap_s.at[s], ap_r.at[src_x], r, c).wait_recv()

    colacc[...] = jnp.zeros(colacc.shape, F32)
    groups = n_a // 128
    to_exp2 = scale * math.log2(math.e)

    def first(j, carry):
        cells = desc_a[j]
        rows = [jnp.zeros((1, 128), F32) for _ in range(groups)]
        for k in range(KMAX):
            found = lax.dot_general(
                desc_b[k], cells, (((1,), (1,)), ((), ())), preferred_element_type=F32
            )
            scores[k, j] = found
            acc = jnp.zeros((n_b, 128), F32)
            for g in range(groups):
                weights = jnp.exp2(found[:, g * 128 : (g + 1) * 128] * to_exp2)
                acc = acc + weights
                part = jnp.sum(weights, axis=0, keepdims=True)
                rows[g] = rows[g] + jnp.where(live[k], part, 0.0)
            colacc[k] = colacc[k] + acc
        rowpart[j] = jnp.concatenate(rows + rows, axis=0)
        return carry

    lax.fori_loop(0, n_col, first, 0)

    which = lax.broadcasted_iota(jnp.int32, (n_col, n_b), 0)
    own = jnp.zeros((n_col, n_b), F32)
    for k in range(KMAX):
        line = jnp.sum(colacc[k].T, axis=0, keepdims=True)
        own = own + jnp.where((which == listed[k]) & live[k], line, 0.0)
    coly[y] = own
    for s in (2, 1, 3):
        go(remote(coly.at[y], coly.at[y], cy_s.at[s], cy_r.at[y], yrow(s), c))
    for s in range(1, n_col):
        far = (c + s) % n_col
        go(remote(rowpart.at[far], rowrecv.at[c], rs_s.at[s], rs_r.at[c], r, far))
    rowrecv[c] = rowpart[c]
    for s in (1, 3, 2):
        src = (y + s) % NY
        slot = coly.at[src]
        remote(slot, slot, cy_s.at[s], cy_r.at[src], r, c).wait_recv()
    colz[z] = jnp.sum(coly[...], axis=0)
    for s in zs:
        go(remote(colz.at[z], colz.at[z], cz_s.at[s], cz_r.at[z], zrow(s), c))
    for s in (1, 7, 2, 6, 3, 5, 4):
        src = (z + s) % nz
        slot = colz.at[src]
        remote(slot, slot, cz_s.at[s], cz_r.at[src], r, c).wait_recv()
    logs = jnp.log(jnp.sum(colz[...], axis=0))
    logfull[...] = logs
    per = 128 // STRIP
    chunk = pl.ds(pl.multiple_of((r // per) * 128, 128), 128)
    lchunk[...] = logfull[:, chunk]
    lrecv[c] = lchunk[...]
    for s in range(1, n_col):
        far = (c + s) % n_col
        go(remote(lchunk, lrecv.at[c], lg_s.at[s], lg_r.at[c], r, far))

    lower = []
    for k in range(KMAX):
        line = jnp.sum(jnp.where(which == listed[k], logs, 0.0), axis=0, keepdims=True)
        lower.append(jnp.broadcast_to(line * (0.5 / scale), (128, n_b)).T)
    for k in range(KMAX):
        colacc[k] = lower[k]

    def second(j, carry):
        best = [jnp.full((1, 128), -jnp.inf, F32) for _ in range(groups)]
        for k in range(KMAX):
            for g in range(groups):
                candidate = scores[k, j, :, pl.ds(g * 128, 128)] - colacc[k]
                top_of = jnp.max(candidate, axis=0, keepdims=True)
                best[g] = jnp.maximum(best[g], jnp.where(live[k], top_of, -jnp.inf))
        maxpart[j] = jnp.concatenate(best + best, axis=0)
        return carry

    lax.fori_loop(0, n_col, second, 0)
    for s in range(1, n_col):
        far = (c + s) % n_col
        go(remote(maxpart.at[far], maxrecv.at[c], mx_s.at[s], mx_r.at[c], r, far))
    maxrecv[c] = maxpart[c]

    for s in range(1, n_col):
        src = (c + n_col - s) % n_col
        remote(rowpart.at[src], rowrecv.at[src], rs_s.at[s], rs_r.at[src], r, c).wait_recv()
        remote(lchunk, lrecv.at[src], lg_s.at[s], lg_r.at[src], r, c).wait_recv()
    row_log = jnp.log(jnp.sum(rowrecv[...], axis=0))
    lane = lax.broadcasted_iota(jnp.int32, (n_col, 128), 1)
    sub = lax.broadcasted_iota(jnp.int32, (n_col, 128), 0)
    out = jnp.zeros((n_col, 128), F32)
    for j in range(n_col):
        shift = (STRIP * j + 128 - STRIP * (r % per)) % 128
        moved = pltpu.roll(lrecv[j], shift, 1)
        out = out + jnp.where((lane // STRIP == j) & (sub == c), moved, 0.0)
    logs_out[...] = jnp.sum(out, axis=0, keepdims=True)
    for s in range(1, n_col):
        src = (c + n_col - s) % n_col
        remote(maxpart.at[src], maxrecv.at[src], mx_s.at[s], mx_r.at[src], r, c).wait_recv()
    best = jnp.max(maxrecv[...], axis=0) * (2.0 * scale) - row_log
    conf_out[...] = best[0:4]
    for copy in sends:
        copy.wait_send()


def local(feat_a, feat_b, conv_weight, conv_bias, pair_lists, pair_counts):
    n_row = lax.axis_size("row")
    n_col = lax.axis_size("col")
    ch = feat_a.shape[2]
    width = feat_a.shape[1]
    desc = conv_weight.shape[3]
    n_a = feat_a.shape[0] * width
    n_b = n_row * STRIP
    nz = n_row // NY
    nx = n_col // 2
    scale = 1.0 / (desc * 0.1)
    vmem = pl.BlockSpec(memory_space=pltpu.VMEM)
    smem = pl.BlockSpec(memory_space=pltpu.SMEM)
    dma = pltpu.SemaphoreType.DMA
    scratch = [
        pltpu.VMEM((2, width, ch), BF16),
        pltpu.VMEM((2, 6, STRIP, ch), BF16),
        pltpu.VMEM((n_col, width, ch), BF16),
        pltpu.VMEM((n_col + 1, STRIP, ch), BF16),
        pltpu.VMEM((n_row, n_col + 1, STRIP, ch), BF16),
        pltpu.VMEM((6, width, 3 * ch), BF16),
        pltpu.VMEM((n_row + 2, STRIP, 3 * ch), BF16),
        pltpu.VMEM((n_col, n_a, desc), BF16),
        pltpu.VMEM((KMAX, n_b, desc), BF16),
        pltpu.VMEM((KMAX, n_col, n_b, n_a), F32),
        pltpu.VMEM((KMAX, n_b, 128), F32),
        pltpu.VMEM((NY, n_col, n_b), F32),
        pltpu.VMEM((nz, n_col, n_b), F32),
        pltpu.VMEM((n_col, 128), F32),
        pltpu.VMEM((n_col, n_col, 128), F32),
        pltpu.VMEM((n_col, n_b), F32),
    ]
    scratch += [pltpu.VMEM((n_col, 8, 128), F32)] * 4
    for shape in (
        (8,), (n_col,), (nz,), (nz, NY), (nx,), (nx,), (NY,), (nz,),
        (n_col,), (n_col,), (n_col,),
    ):
        received = (nz, NY) if shape == (nz, NY) else shape
        scratch += [dma(shape), dma(received)]
    run = pl.pallas_call(
        functools.partial(kernel, n_row, n_col, scale),
        out_shape=(
            jax.ShapeDtypeStruct((4, 128), F32),
            jax.ShapeDtypeStruct((1, 128), F32),
        ),
        in_specs=[vmem, vmem, vmem, vmem, smem, smem],
        out_specs=(vmem, vmem),
        scratch_shapes=scratch,
        compiler_params=pltpu.CompilerParams(
            collective_id=0, has_side_effects=True, vmem_limit_bytes=56 * 1024 * 1024
        ),
    )
    conf, logs = run(
        feat_a,
        feat_b.reshape(feat_b.shape[1], ch),
        conv_weight.reshape(3, 3 * ch, desc),
        conv_bias.reshape(1, desc),
        pair_lists,
        pair_counts,
    )
    return (conf, logs)


def solution(mesh):
    in_specs = (P("row", "col", None), P("row", "col", None), P(), P(), P(), P())
    out_specs = (P("row", "col"), P("row", "col"))
    return jax.shard_map(local, mesh=mesh, in_specs=in_specs, out_specs=out_specs, check_vma=False)
```

time: 479 us -> 65.3 us (0.14)
  waiting for transfers between devices: 380 us -> 0 us
  Pallas kernels: 0 us -> 61.4 us
  matrix products: 27 us -> 0 us
  starting transfers between devices: 22.2 us -> 0 us
  other arithmetic: 20.7 us -> 0 us
  between operations: 20.5 us -> 0.66 us
    psum x2 -> x0, waiting for transfers between devices: 318 us -> none  [the longest x1 243 us: local(): col_all = lax.psum(col_tot, ('row', 'col'))]
    pallas_call x0 -> x1, Pallas kernels: none -> 61.4 us  [local(): run(feat_a, feat_b.reshape(feat_b.shape[1], ch), conv_weight.reshape(3, 3...]
    all_gather x1 -> x0, waiting for transfers between devices: 57.2 us -> none  [local(): own_block = lax.all_gather(unit_b, 'row', axis=0, tiled=True)]
    dot_general x34 -> x0, matrix products: 27 us -> none  [the longest x16 17.3 us: accumulate(): jnp.einsum('nd,md->nm', unit_a, piece, preferred_element_type=jnp.float32)]
    ppermute x8 -> x0, starting transfers between devices: 22.1 us -> none  [the longest x4 13.6 us: with_halo(): lax.ppermute(tail, axis, [(i, (i + 1) % count) for i in range(ends)])]
    add x9 -> x0, other arithmetic: 8.79 us -> none  [the longest x8 8.79 us: accumulate(): return (row_sum + jnp.sum(weights, axis=1), jnp.sum(weights, axis=0))]
    max x9 -> x0, other arithmetic: 5.76 us -> none  [the longest x8 4.49 us: accumulate(): return (jnp.maximum(running, candidate), None)]
  transfers between devices with their start and end apart: 11 -> 0, of which waited for: 5 -> 0; matrix products, arithmetic and copies ran while one was open for 2% -> 0% of each run, Pallas kernels for 0% -> 0%
where the time goes in v1:
time: 65.3 us; the launch traced here: 65.2 us
  Pallas kernels  61.4 us (94%)
  local copies, waits for them, and re-layouts  3.12 us (5%)
  between operations  0.66 us (1%)
    pallas_call x1, Pallas kernels, local(): run(feat_a, feat_b.reshape(feat_b.shape[1], ch), conv_weight.reshape(3, 3...  61.4 us
    unnamed x9, local copies, waits for them, and re-layouts  3.12 us

profile of v1, /device:TPU:1, one launch (start us, length us, event | category | flops | bytes accessed | tf_op | source)
XLA Modules:
  0.0 65.2 jit_solution(4018836658578158124)
XLA Ops:
  0.6 0.0 copy-start.1
  0.6 0.7 %copy-done.1 = s32[32,2]{0,1:T(2,128)S(1)} copy-done((s32[32,2]{0,1:T(2,128)S(1)}, s32[32,2]{0,1:T(2,128)}, u32[]{:S(2)}) %copy-start.1) | copy-done | bytes 280
  1.3 0.7 %copy.8.lists = s32[32,2]{1,0:T(8,128)} copy(s32[32,2]{0,1:T(2,128)S(1)} %copy-done.1) | data formatting | bytes 512 | tf_op args[4]
  2.0 61.4 %shard_map.77 = (f32[4,128]{1,0:T(4,128)}, f32[1,128]{1,0:T(1,128)}) custom-call(bf16[4,128,128]{2,1,0:T(8,128)(2,1)} %feat_a.1, bf16[128,128]{1,0:T(8,128)(2,1)} %bitcast.4, bf16[3,384,256]{2,1,0:T(8,128)(2,1)} %bitcast.3, f32[1,256]{1,0:T(1,128)} %bitcast.5, s32[32,2]{1,0:T(8,128)} %copy.8.lists, s32[32]{0:T(128)} %counts.1), custom_call_target="tpu_custom_call" | custom-call | tf_op jit(solution)/shard_map/pallas_call | solution.py:363
  63.4 0.0 copy-start
  63.4 0.7 %copy-done = f32[4,128]{1,0:T(4,128)S(1)} copy-done((f32[4,128]{1,0:T(4,128)S(1)}, f32[4,128]{1,0:T(4,128)}, u32[]{:S(2)}) %copy-start) | copy-done | bytes 2072
  64.1 0.0 copy-start.2
  64.1 0.6 copy.11
  64.6 0.0 copy-done.2
  64.7 0.5 copy.12
Async XLA Ops:
  0.6 0.7 %copy-start.1 = (s32[32,2]{0,1:T(2,128)S(1)}, s32[32,2]{0,1:T(2,128)}, u32[]{:S(2)}) copy-start(s32[32,2]{0,1:T(2,128)} %param.10) | copy-start | bytes 772
  63.4 0.7 %copy-start = (f32[4,128]{1,0:T(4,128)S(1)}, f32[4,128]{1,0:T(4,128)}, u32[]{:S(2)}) copy-start(f32[4,128]{1,0:T(4,128)} %get-tuple-element.4) | copy-start | bytes 6148
  64.1 0.6 copy-start.2

commit v2 on v1

--- a/solution.py
+++ b/solution.py
@@ -48,14 +48,14 @@
 
 def kernel(
     n_row, n_col, scale,
-    feat_a, feat_b, weight, bias, lists, counts,
+    feat_a_in, feat_b_in, weight_in, bias_in, lists, counts,
     conf_out, logs_out,
-    hrow, hcol, brow, unit, ball, taps_a, taps_b, desc_a, desc_b,
+    feat_a, tiles, weight, bias, hrow, hcol, brow, unit, ball, taps_a, taps_b, desc_a, desc_b,
     scores, colacc, coly, colz, lchunk, lrecv, logfull,
     rowpart, rowrecv, maxpart, maxrecv,
     halo_s, halo_r, bx_s, bx_r, bz_s, bz_r, by_s, by_r,
     ax_s, ax_r, ap_s, ap_r, cy_s, cy_r, cz_s, cz_r,
-    rs_s, rs_r, lg_s, lg_r, mx_s, mx_r,
+    rs_s, rs_r, lg_s, lg_r, mx_s, mx_r, in_sem,
 ):
     r = lax.axis_index("row")
     c = lax.axis_index("col")
@@ -76,6 +76,22 @@
     def yrow(step):
         return z * NY + (y + step) % NY
 
+    tail = pl.ds(n_col - 1, 1)
+    fetches = [
+        pltpu.make_async_copy(src, dst, in_sem.at[i])
+        for i, (src, dst) in enumerate(
+            [
+                (feat_b_in, tiles.at[pl.ds(1, n_col)]),
+                (feat_b_in.at[tail], tiles.at[pl.ds(0, 1)]),
+                (feat_b_in.at[pl.ds(0, 1)], tiles.at[pl.ds(n_col + 1, 1)]),
+                (feat_a_in, feat_a),
+                (weight_in, weight),
+                (bias_in, bias),
+            ]
+        )
+    ]
+    for fetch in fetches:
+        fetch.start()
     barrier = pltpu.get_barrier_semaphore()
     partners = [(r, (c + s) % n_col) for s in range(1, n_col)]
     partners += [(yrow(s), c) for s in range(1, NY)]
@@ -92,53 +108,84 @@
         sends.append(copy)
         return copy
 
-    bx = []
-    for s in range(1, n_col):
-        bx.append(
-            go(remote(feat_b, brow.at[c], bx_s.at[s], bx_r.at[c], r, (c + s) % n_col))
-        )
+    for fetch in fetches[:3]:
+        fetch.wait()
+    brow[c] = tiles[pl.ds(c, 3)]
+    for s in range(1, n_col):
+        far = (c + s) % n_col
+        go(remote(tiles.at[pl.ds(far, 3)], brow.at[c], bx_s.at[s], bx_r.at[c], r, far))
     last = feat_a.shape[1] - STRIP
     edges = [
-        (feat_a.at[3], hrow.at[0], down, c),
-        (feat_a.at[0], hrow.at[1], up, c),
-        (feat_a.at[:, pl.ds(last, STRIP)], hcol.at[0, pl.ds(1, 4)], r, rt),
-        (feat_a.at[:, pl.ds(0, STRIP)], hcol.at[1, pl.ds(1, 4)], r, lf),
-        (feat_a.at[3, pl.ds(last, STRIP)], hcol.at[0, 0], down, rt),
-        (feat_a.at[3, pl.ds(0, STRIP)], hcol.at[1, 0], down, lf),
-        (feat_a.at[0, pl.ds(last, STRIP)], hcol.at[0, 5], up, rt),
-        (feat_a.at[0, pl.ds(0, STRIP)], hcol.at[1, 5], up, lf),
+        (feat_a_in.at[3], hrow.at[0], down, c),
+        (feat_a_in.at[0], hrow.at[1], up, c),
+        (feat_a_in.at[:, pl.ds(last, STRIP)], hcol.at[0, pl.ds(1, 4)], r, rt),
+        (feat_a_in.at[:, pl.ds(0, STRIP)], hcol.at[1, pl.ds(1, 4)], r, lf),
+        (feat_a_in.at[3, pl.ds(last, STRIP)], hcol.at[0, 0], down, rt),
+        (feat_a_in.at[3, pl.ds(0, STRIP)], hcol.at[1, 0], down, lf),
+        (feat_a_in.at[0, pl.ds(last, STRIP)], hcol.at[0, 5], up, rt),
+        (feat_a_in.at[0, pl.ds(0, STRIP)], hcol.at[1, 5], up, lf),
     ]
     halos = [
         go(remote(src, dst, halo_s.at[i], halo_r.at[i], row, col))
         for i, (src, dst, row, col) in enumerate(edges)
     ]
 
-    brow[c] = feat_b[...]
     for s in range(1, n_col):
         src = (c + n_col - s) % n_col
-        remote(feat_b, brow.at[src], bx_s.at[s], bx_r.at[src], r, src).wait_recv()
-
-    strip = pl.ds(pl.multiple_of(c * STRIP, STRIP), STRIP)
-    width = feat_b.shape[0]
-    unit[pl.ds(0, n_col)] = brow[:, strip, :]
-    entry = lax.broadcasted_iota(jnp.int32, (2 * n_col, n_col * width), 0)
-    column = lax.broadcasted_iota(jnp.int32, (2 * n_col, n_col * width), 1)
+        mine = brow.at[src]
+        remote(mine, mine, bx_s.at[s], bx_r.at[src], r, src).wait_recv()
+
+    unit[pl.ds(0, n_col)] = brow[:, 1]
+    entry = lax.broadcasted_iota(jnp.int32, (2 * n_col, n_col * 3 * STRIP), 0)
+    column = lax.broadcasted_iota(jnp.int32, (2 * n_col, n_col * 3 * STRIP), 1)
+    at_start = jnp.where(c == 0, 1, 0)
+    at_end = jnp.where(c == n_col - 1, 1, 0)
     wanted = jnp.where(
         entry < n_col,
-        entry * width + c * STRIP - 1,
-        (entry - n_col) * width + c * STRIP + STRIP,
+        (entry - at_start) * 3 * STRIP + STRIP - 1,
+        (entry - n_col + at_end) * 3 * STRIP + 2 * STRIP,
     )
     pick = jnp.where(column == wanted, 1.0, 0.0).astype(BF16)
-    row_all = brow[...].reshape(n_col * width, brow.shape[2])
+    row_all = brow[...].reshape(n_col * 3 * STRIP, brow.shape[3])
     unit[n_col] = jnp.dot(pick, row_all, preferred_element_type=F32).astype(BF16)
 
-    zs = [4, 3, 5, 2, 6, 1, 7]
-    for s in zs:
-        go(remote(unit, ball.at[r], bz_s.at[s], bz_r.at[z], zrow(s), c))
-    for s in range(1, NY):
-        go(remote(unit, ball.at[r], by_s.at[0, s], by_r.at[z, y], yrow(s), c))
+    d = 1 - 2 * core
+    zup, zdown, yup, ydown = zrow(1), zrow(nz - 1), yrow(1), yrow(NY - 1)
+    own = ball.at[r]
+    go(remote(unit, own, bz_s.at[0, 0], bz_r.at[z], zup, c))
+    go(remote(unit, own, bz_s.at[1, 0], bz_r.at[z], zdown, c))
+    go(remote(unit, own, by_s.at[0, z], by_r.at[z, y], yup, c))
+    go(remote(unit, own, by_s.at[1, z], by_r.at[z, y], ydown, c))
     ball[r] = unit[...]
 
+    def z_arrived(step):
+        src_z = (z + step + nz) % nz
+        slot = ball.at[src_z * NY + y]
+        remote(slot, slot, bz_s.at[0, 0], bz_r.at[src_z], r, c).wait_recv()
+        return src_z, slot
+
+    def z_forward(slot, src_z, way, to, hop):
+        go(remote(slot, slot, bz_s.at[way, hop], bz_r.at[src_z], to, c))
+
+    def y_forward(slot, src_z):
+        go(remote(slot, slot, by_s.at[0, src_z], by_r.at[src_z, y], yup, c))
+        go(remote(slot, slot, by_s.at[1, src_z], by_r.at[src_z, y], ydown, c))
+
+    def y_arrived(step, src_y):
+        src_z = (z + step + nz) % nz
+        slot = ball.at[src_z * NY + src_y]
+        remote(slot, slot, by_s.at[0, 0], by_r.at[src_z, src_y], r, c).wait_recv()
+        return src_z, slot
+
+    def y_relay(step):
+        src_y = (y - d + NY) % NY
+        src_z, slot = y_arrived(step, src_y)
+        to = z * NY + (y + d + NY) % NY
+        go(remote(slot, slot, by_s.at[2, src_z], by_r.at[src_z, src_y], to, c))
+
+    fetches[3].wait()
+    fetches[4].wait()
+    fetches[5].wait()
     for i, (src, dst, row, col) in enumerate(edges):
         halos[i].wait_recv()
     zero = jnp.zeros((), F32)
@@ -157,28 +204,51 @@
         total = total + jnp.dot(window, weight[i], preferred_element_type=F32)
     desc_a[c] = normalized(total, bias[...])
     mate = x * 2 + (1 - core)
-    for s in (2, 1, 3):
-        far = ((x + s) % nx) * 2 + core
-        go(remote(desc_a.at[c], desc_a.at[c], ax_s.at[s], ax_r.at[x], r, far))
-    go(remote(desc_a.at[c], desc_a.at[c], ap_s.at[0], ap_r.at[x], r, mate))
-
-    for i, s in enumerate((1, 7, 2, 6, 3, 5, 4)):
-        src_z = (z + s) % nz
-        slot = ball.at[src_z * NY + y]
-        remote(unit, slot, bz_s.at[s], bz_r.at[src_z], r, c).wait_recv()
-        for t in range(1, NY):
-            go(remote(slot, slot, by_s.at[i + 1, t], by_r.at[src_z, y], yrow(t), c))
-    for s in (1, 3, 2):
-        src_x = (x + s) % nx
+    mine = desc_a.at[c]
+    xup = ((x + 1) % nx) * 2 + core
+    xdown = ((x + nx - 1) % nx) * 2 + core
+    xnext = ((x + d + nx) % nx) * 2 + core
+    go(remote(mine, mine, ax_s.at[0], ax_r.at[x], r, xup))
+    go(remote(mine, mine, ax_s.at[1], ax_r.at[x], r, xdown))
+    go(remote(mine, mine, ap_s.at[0], ap_r.at[x], r, mate))
+
+    def x_arrived(step, hop):
+        src_x = (x + step + nx) % nx
         slot = desc_a.at[src_x * 2 + core]
-        remote(slot, slot, ax_s.at[s], ax_r.at[src_x], r, c).wait_recv()
-        go(remote(slot, slot, ap_s.at[s], ap_r.at[src_x], r, mate))
-    for s in (0, 1, 7, 2, 6, 3, 5, 4):
-        src_z = (z + s) % nz
-        for t in range(1, NY):
-            src_y = (y + t) % NY
-            slot = ball.at[src_z * NY + src_y]
-            remote(slot, slot, by_s.at[0, t], by_r.at[src_z, src_y], r, c).wait_recv()
+        remote(slot, slot, ax_s.at[0], ax_r.at[src_x], r, c).wait_recv()
+        if hop == 1:
+            go(remote(slot, slot, ax_s.at[2], ax_r.at[src_x], r, xnext))
+        go(remote(slot, slot, ap_s.at[hop], ap_r.at[src_x], r, mate))
+
+    for hop in (1, 2):
+        for way, step, to in ((0, -hop, zup), (1, hop, zdown)):
+            src_z, slot = z_arrived(step)
+            z_forward(slot, src_z, way, to, hop)
+            y_forward(slot, src_z)
+        if hop == 1:
+            y_relay(0)
+        else:
+            y_relay(-1)
+            y_relay(1)
+    z_up = (z + d + nz) % nz
+    src_z, slot = z_arrived(-3 * d)
+    z_forward(slot, src_z, 0, z_up * NY + y, 3)
+    y_forward(slot, src_z)
+    src_z, slot = z_arrived(3 * d)
+    y_forward(slot, src_z)
+    x_arrived(-d, 1)
+    y_relay(-2)
+    y_relay(2)
+    x_arrived(d, 2)
+    src_z, slot = z_arrived(4)
+    y_forward(slot, src_z)
+    y_relay(-3)
+    y_relay(3)
+    y_relay(4)
+    x_arrived(2, 3)
+    for step in (0, -1, 1, -2, 2, -3, 3, 4):
+        y_arrived(step, (y + d + NY) % NY)
+        y_arrived(step, (y + 2) % NY)
 
     listed = [lists[r, k] for k in range(KMAX)]
     live = [counts[r] > k for k in range(KMAX)]
@@ -247,7 +317,7 @@
         slot = coly.at[src]
         remote(slot, slot, cy_s.at[s], cy_r.at[src], r, c).wait_recv()
     colz[z] = jnp.sum(coly[...], axis=0)
-    for s in zs:
+    for s in (4, 3, 5, 2, 6, 1, 7):
         go(remote(colz.at[z], colz.at[z], cz_s.at[s], cz_r.at[z], zrow(s), c))
     for s in (1, 7, 2, 6, 3, 5, 4):
         src = (z + s) % nz
@@ -320,12 +390,17 @@
     nx = n_col // 2
     scale = 1.0 / (desc * 0.1)
     vmem = pl.BlockSpec(memory_space=pltpu.VMEM)
+    hbm = pl.BlockSpec(memory_space=pl.ANY)
     smem = pl.BlockSpec(memory_space=pltpu.SMEM)
     dma = pltpu.SemaphoreType.DMA
     scratch = [
+        pltpu.VMEM(feat_a.shape, BF16),
+        pltpu.VMEM((n_col + 2, STRIP, ch), BF16),
+        pltpu.VMEM((3, 3 * ch, desc), BF16),
+        pltpu.VMEM((1, desc), F32),
         pltpu.VMEM((2, width, ch), BF16),
         pltpu.VMEM((2, 6, STRIP, ch), BF16),
-        pltpu.VMEM((n_col, width, ch), BF16),
+        pltpu.VMEM((n_col, 3, STRIP, ch), BF16),
         pltpu.VMEM((n_col + 1, STRIP, ch), BF16),
         pltpu.VMEM((n_row, n_col + 1, STRIP, ch), BF16),
         pltpu.VMEM((6, width, 3 * ch), BF16),
@@ -341,19 +416,28 @@
         pltpu.VMEM((n_col, n_b), F32),
     ]
     scratch += [pltpu.VMEM((n_col, 8, 128), F32)] * 4
-    for shape in (
-        (8,), (n_col,), (nz,), (nz, NY), (nx,), (nx,), (NY,), (nz,),
-        (n_col,), (n_col,), (n_col,),
+    for sent, received in (
+        ((8,), (8,)),
+        ((n_col,), (n_col,)),
+        ((2, 4), (nz,)),
+        ((3, nz), (nz, NY)),
+        ((3,), (nx,)),
+        ((nx,), (nx,)),
+        ((NY,), (NY,)),
+        ((nz,), (nz,)),
+        ((n_col,), (n_col,)),
+        ((n_col,), (n_col,)),
+        ((n_col,), (n_col,)),
     ):
-        received = (nz, NY) if shape == (nz, NY) else shape
-        scratch += [dma(shape), dma(received)]
+        scratch += [dma(sent), dma(received)]
+    scratch.append(dma((6,)))
     run = pl.pallas_call(
         functools.partial(kernel, n_row, n_col, scale),
         out_shape=(
             jax.ShapeDtypeStruct((4, 128), F32),
             jax.ShapeDtypeStruct((1, 128), F32),
         ),
-        in_specs=[vmem, vmem, vmem, vmem, smem, smem],
+        in_specs=[hbm, hbm, hbm, hbm, smem, smem],
         out_specs=(vmem, vmem),
         scratch_shapes=scratch,
         compiler_params=pltpu.CompilerParams(
@@ -362,7 +446,7 @@
     )
     conf, logs = run(
         feat_a,
-        feat_b.reshape(feat_b.shape[1], ch),
+        feat_b.reshape(width // STRIP, STRIP, ch),
         conv_weight.reshape(3, 3 * ch, desc),
         conv_bias.reshape(1, desc),
         pair_lists,

time: 65.3 us -> 61.3 us (0.939)
  Pallas kernels: 61.4 us -> 57.3 us
    pallas_call x1, Pallas kernels: 61.4 us -> 57.3 us  [local(): run(feat_a, feat_b.reshape(width // STRIP, STRIP, ch), conv_weight.reshap...]
where the time goes in v2:
time: 61.3 us; the launch traced here: 61 us
  Pallas kernels  57.3 us (93%)
  local copies, waits for them, and re-layouts  3.12 us (5%)
  between operations  0.66 us (1%)
    pallas_call x1, Pallas kernels, local(): run(feat_a, feat_b.reshape(width // STRIP, STRIP, ch), conv_weight.reshap...  57.3 us
    unnamed x9, local copies, waits for them, and re-layouts  3.12 us

profile of v2, /device:TPU:1, one launch (start us, length us, event | category | flops | bytes accessed | tf_op | source)
XLA Modules:
  0.0 61.0 jit_solution(14361221361929123170)
XLA Ops:
  0.6 0.0 copy-start.1
  0.6 0.7 %copy-done.1 = s32[32,2]{0,1:T(2,128)S(1)} copy-done((s32[32,2]{0,1:T(2,128)S(1)}, s32[32,2]{0,1:T(2,128)}, u32[]{:S(2)}) %copy-start.1) | copy-done | bytes 280
  1.3 0.7 %copy.8.lists = s32[32,2]{1,0:T(8,128)} copy(s32[32,2]{0,1:T(2,128)S(1)} %copy-done.1) | data formatting | bytes 512 | tf_op args[4]
  2.0 57.3 %shard_map.77 = (f32[4,128]{1,0:T(4,128)}, f32[1,128]{1,0:T(1,128)}) custom-call(bf16[4,128,128]{2,1,0:T(8,128)(2,1)} %feat_a_in.1, bf16[8,16,128]{2,1,0:T(8,128)(2,1)} %bitcast.4, bf16[3,384,256]{2,1,0:T(8,128)(2,1)} %bitcast.3, f32[1,256]{1,0:T(1,128)} %bitcast.5, s32[32,2]{1,0:T(8,128)} %copy.8.lists, s32[32]{0:T(128)} %counts.1), custom_call_target="tpu_custom_call" | custom-call | tf_op jit(solution)/shard_map/pallas_call | solution.py:447
  59.3 0.0 copy-start
  59.3 0.7 %copy-done = f32[4,128]{1,0:T(4,128)S(1)} copy-done((f32[4,128]{1,0:T(4,128)S(1)}, f32[4,128]{1,0:T(4,128)}, u32[]{:S(2)}) %copy-start) | copy-done | bytes 2072
  59.9 0.0 copy-start.2
  59.9 0.6 copy.11
  60.5 0.0 copy-done.2
  60.5 0.5 copy.12
Async XLA Ops:
  0.6 0.7 %copy-start.1 = (s32[32,2]{0,1:T(2,128)S(1)}, s32[32,2]{0,1:T(2,128)}, u32[]{:S(2)}) copy-start(s32[32,2]{0,1:T(2,128)} %param.10) | copy-start | bytes 772
  59.3 0.7 %copy-start = (f32[4,128]{1,0:T(4,128)S(1)}, f32[4,128]{1,0:T(4,128)}, u32[]{:S(2)}) copy-start(f32[4,128]{1,0:T(4,128)} %get-tuple-element.4) | copy-start | bytes 6148
  59.9 0.6 copy-start.2

commit v3 on v2

--- a/solution.py
+++ b/solution.py
@@ -49,13 +49,13 @@
 def kernel(
     n_row, n_col, scale,
     feat_a_in, feat_b_in, weight_in, bias_in, lists, counts,
-    conf_out, logs_out,
+    out_ref,
     feat_a, tiles, weight, bias, hrow, hcol, brow, unit, ball, taps_a, taps_b, desc_a, desc_b,
-    scores, colacc, coly, colz, lchunk, lrecv, logfull,
+    scores, colacc, colown, coly, colz, lchunk, lrecv, logfull,
     rowpart, rowrecv, maxpart, maxrecv,
     halo_s, halo_r, bx_s, bx_r, bz_s, bz_r, by_s, by_r,
     ax_s, ax_r, ap_s, ap_r, cy_s, cy_r, cz_s, cz_r,
-    rs_s, rs_r, lg_s, lg_r, mx_s, mx_r, in_sem,
+    rs_s, rs_r, lg_s, lg_r, mx_s, mx_r, cl_s, cl_r, in_sem,
 ):
     r = lax.axis_index("row")
     c = lax.axis_index("col")
@@ -94,8 +94,7 @@
         fetch.start()
     barrier = pltpu.get_barrier_semaphore()
     partners = [(r, (c + s) % n_col) for s in range(1, n_col)]
-    partners += [(yrow(s), c) for s in range(1, NY)]
-    partners += [(zrow(s), c) for s in range(1, nz)]
+    partners += [(yrow(1), c), (yrow(NY - 1), c), (zrow(1), c), (zrow(nz - 1), c)]
     partners += [(v, h) for v in (up, down) for h in (lf, c, rt)]
     for device in partners:
         pl.semaphore_signal(barrier, inc=1, device_id=device, device_id_type=MESH)
@@ -250,7 +249,7 @@
         y_arrived(step, (y + d + NY) % NY)
         y_arrived(step, (y + 2) % NY)
 
-    listed = [lists[r, k] for k in range(KMAX)]
+    listed = [lists[k, r] for k in range(KMAX)]
     live = [counts[r] > k for k in range(KMAX)]
     n_h = n_row
     n_b = n_h * STRIP
@@ -305,9 +304,12 @@
     for k in range(KMAX):
         line = jnp.sum(colacc[k].T, axis=0, keepdims=True)
         own = own + jnp.where((which == listed[k]) & live[k], line, 0.0)
-    coly[y] = own
+    for q in range(NY):
+        colown[q] = own[:, q * 128 : (q + 1) * 128]
+    coly[y] = colown[y]
     for s in (2, 1, 3):
-        go(remote(coly.at[y], coly.at[y], cy_s.at[s], cy_r.at[y], yrow(s), c))
+        q = (y + s) % NY
+        go(remote(colown.at[q], coly.at[y], cy_s.at[s], cy_r.at[y], yrow(s), c))
     for s in range(1, n_col):
         far = (c + s) % n_col
         go(remote(rowpart.at[far], rowrecv.at[c], rs_s.at[s], rs_r.at[c], r, far))
@@ -323,11 +325,17 @@
         src = (z + s) % nz
         slot = colz.at[src]
         remote(slot, slot, cz_s.at[s], cz_r.at[src], r, c).wait_recv()
-    logs = jnp.log(jnp.sum(colz[...], axis=0))
-    logfull[...] = logs
+    logfull[y] = jnp.log(jnp.sum(colz[...], axis=0))
+    for s in (2, 1, 3):
+        mine = logfull.at[y]
+        go(remote(mine, mine, cl_s.at[s], cl_r.at[y], yrow(s), c))
+    for s in (1, 3, 2):
+        src = (y + s) % NY
+        slot = logfull.at[src]
+        remote(slot, slot, cl_s.at[s], cl_r.at[src], r, c).wait_recv()
+    logs = jnp.concatenate([logfull[q] for q in range(NY)], axis=1)
     per = 128 // STRIP
-    chunk = pl.ds(pl.multiple_of((r // per) * 128, 128), 128)
-    lchunk[...] = logfull[:, chunk]
+    lchunk[...] = logfull[r // per]
     lrecv[c] = lchunk[...]
     for s in range(1, n_col):
         far = (c + s) % n_col
@@ -368,12 +376,12 @@
         shift = (STRIP * j + 128 - STRIP * (r % per)) % 128
         moved = pltpu.roll(lrecv[j], shift, 1)
         out = out + jnp.where((lane // STRIP == j) & (sub == c), moved, 0.0)
-    logs_out[...] = jnp.sum(out, axis=0, keepdims=True)
+    out = jnp.sum(out, axis=0, keepdims=True)
     for s in range(1, n_col):
         src = (c + n_col - s) % n_col
         remote(maxpart.at[src], maxrecv.at[src], mx_s.at[s], mx_r.at[src], r, c).wait_recv()
     best = jnp.max(maxrecv[...], axis=0) * (2.0 * scale) - row_log
-    conf_out[...] = best[0:4]
+    out_ref[...] = jnp.concatenate([best[0:4], jnp.broadcast_to(out, (4, 128))], axis=0)
     for copy in sends:
         copy.wait_send()
 
@@ -409,11 +417,12 @@
         pltpu.VMEM((KMAX, n_b, desc), BF16),
         pltpu.VMEM((KMAX, n_col, n_b, n_a), F32),
         pltpu.VMEM((KMAX, n_b, 128), F32),
-        pltpu.VMEM((NY, n_col, n_b), F32),
-        pltpu.VMEM((nz, n_col, n_b), F32),
+        pltpu.VMEM((NY, n_col, 128), F32),
+        pltpu.VMEM((NY, n_col, 128), F32),
+        pltpu.VMEM((nz, n_col, 128), F32),
         pltpu.VMEM((n_col, 128), F32),
         pltpu.VMEM((n_col, n_col, 128), F32),
-        pltpu.VMEM((n_col, n_b), F32),
+        pltpu.VMEM((NY, n_col, 128), F32),
     ]
     scratch += [pltpu.VMEM((n_col, 8, 128), F32)] * 4
     for sent, received in (
@@ -428,31 +437,29 @@
         ((n_col,), (n_col,)),
         ((n_col,), (n_col,)),
         ((n_col,), (n_col,)),
+        ((NY,), (NY,)),
     ):
         scratch += [dma(sent), dma(received)]
     scratch.append(dma((6,)))
     run = pl.pallas_call(
         functools.partial(kernel, n_row, n_col, scale),
-        out_shape=(
-            jax.ShapeDtypeStruct((4, 128), F32),
-            jax.ShapeDtypeStruct((1, 128), F32),
-        ),
+        out_shape=jax.ShapeDtypeStruct((8, 128), F32),
         in_specs=[hbm, hbm, hbm, hbm, smem, smem],
-        out_specs=(vmem, vmem),
+        out_specs=vmem,
         scratch_shapes=scratch,
         compiler_params=pltpu.CompilerParams(
             collective_id=0, has_side_effects=True, vmem_limit_bytes=56 * 1024 * 1024
         ),
     )
-    conf, logs = run(
+    both = run(
         feat_a,
         feat_b.reshape(width // STRIP, STRIP, ch),
         conv_weight.reshape(3, 3 * ch, desc),
         conv_bias.reshape(1, desc),
-        pair_lists,
+        pair_lists.T,
         pair_counts,
     )
-    return (conf, logs)
+    return (both[0:4], both[4:5])
 
 
 def solution(mesh):

time: 61.3 us -> 62.3 us (1.016)
  Pallas kernels: 57.3 us -> 59 us
  local copies, waits for them, and re-layouts: 3.12 us -> 2.45 us
    unnamed x9 -> x0, local copies, waits for them, and re-layouts: 3.12 us -> none
    slice x0 -> x2, local copies, waits for them, and re-layouts: none -> 2.45 us  [local(): return (both[0:4], both[4:5])]
    pallas_call x1, Pallas kernels: 57.3 us -> 59 us  [local(): run(feat_a, feat_b.reshape(width // STRIP, STRIP, ch), conv_weight.reshap...]
where the time goes in v3:
time: 62.3 us; the launch traced here: 62.1 us
  Pallas kernels  59 us (95%)
  local copies, waits for them, and re-layouts  2.45 us (4%)
  between operations  0.64 us (1%)
    pallas_call x1, Pallas kernels, local(): run(feat_a, feat_b.reshape(width // STRIP, STRIP, ch), conv_weight.reshap...  59 us
    slice x2, local copies, waits for them, and re-layouts, local(): return (both[0:4], both[4:5])  2.45 us

profile of v3, /device:TPU:1, one launch (start us, length us, event | category | flops | bytes accessed | tf_op | source)
XLA Modules:
  0.0 62.1 jit_solution(10051011827288306374)
XLA Ops:
  0.6 59.0 %shard_map.77 = f32[8,128]{1,0:T(8,128)} custom-call(bf16[4,128,128]{2,1,0:T(8,128)(2,1)} %feat_a_in.1, bf16[8,16,128]{2,1,0:T(8,128)(2,1)} %bitcast.5, bf16[3,384,256]{2,1,0:T(8,128)(2,1)} %bitcast.4, f32[1,256]{1,0:T(1,128)} %bitcast.6, s32[2,32]{1,0:T(2,128)} %bitcast.7, s32[32]{0:T(128)} %counts.1), custom_call_target="tpu_custom_call" | custom-call | tf_op jit(solution)/shard_map/pallas_call | solution.py:454
  59.6 1.2 %slice.7 = f32[1,128]{1,0:T(1,128)} slice(f32[8,128]{1,0:T(8,128)} %shard_map.77), slice={[4:5], [0:128]} | slice | bytes 1024 | tf_op jit(solution)/shard_map/slice | solution.py:462
  60.8 1.3 %slice.6 = f32[4,128]{1,0:T(4,128)} slice(f32[8,128]{1,0:T(8,128)} %shard_map.77), slice={[0:4], [0:128]} | slice | bytes 4096 | tf_op jit(solution)/shard_map/slice | solution.py:462

commit v4 on v3

--- a/solution.py
+++ b/solution.py
@@ -51,11 +51,11 @@
     feat_a_in, feat_b_in, weight_in, bias_in, lists, counts,
     out_ref,
     feat_a, tiles, weight, bias, hrow, hcol, brow, unit, ball, taps_a, taps_b, desc_a, desc_b,
-    scores, colacc, colown, coly, colz, lchunk, lrecv, logfull,
+    scores, colacc, coly, colz, lchunk, lrecv, logfull,
     rowpart, rowrecv, maxpart, maxrecv,
     halo_s, halo_r, bx_s, bx_r, bz_s, bz_r, by_s, by_r,
     ax_s, ax_r, ap_s, ap_r, cy_s, cy_r, cz_s, cz_r,
-    rs_s, rs_r, lg_s, lg_r, mx_s, mx_r, cl_s, cl_r, in_sem,
+    rs_s, rs_r, lg_s, lg_r, mx_s, mx_r, in_sem,
 ):
     r = lax.axis_index("row")
     c = lax.axis_index("col")
@@ -95,6 +95,7 @@
     barrier = pltpu.get_barrier_semaphore()
     partners = [(r, (c + s) % n_col) for s in range(1, n_col)]
     partners += [(yrow(1), c), (yrow(NY - 1), c), (zrow(1), c), (zrow(nz - 1), c)]
+    partners += [(zrow(2), c), (zrow(nz - 2), c)]
     partners += [(v, h) for v in (up, down) for h in (lf, c, rt)]
     for device in partners:
         pl.semaphore_signal(barrier, inc=1, device_id=device, device_id_type=MESH)
@@ -153,6 +154,8 @@
     own = ball.at[r]
     go(remote(unit, own, bz_s.at[0, 0], bz_r.at[z], zup, c))
     go(remote(unit, own, bz_s.at[1, 0], bz_r.at[z], zdown, c))
+    go(remote(unit, own, bz_s.at[0, 1], bz_r.at[z], zrow(2), c))
+    go(remote(unit, own, bz_s.at[1, 1], bz_r.at[z], zrow(nz - 2), c))
     go(remote(unit, own, by_s.at[0, z], by_r.at[z, y], yup, c))
     go(remote(unit, own, by_s.at[1, z], by_r.at[z, y], ydown, c))
     ball[r] = unit[...]
@@ -182,6 +185,7 @@
         to = z * NY + (y + d + NY) % NY
         go(remote(slot, slot, by_s.at[2, src_z], by_r.at[src_z, src_y], to, c))
 
+    mate = x * 2 + (1 - core)
     fetches[3].wait()
     fetches[4].wait()
     fetches[5].wait()
@@ -202,7 +206,6 @@
         window = taps_a[pl.ds(i, 4)].reshape(n_a, taps_a.shape[2])
         total = total + jnp.dot(window, weight[i], preferred_element_type=F32)
     desc_a[c] = normalized(total, bias[...])
-    mate = x * 2 + (1 - core)
     mine = desc_a.at[c]
     xup = ((x + 1) % nx) * 2 + core
     xdown = ((x + nx - 1) % nx) * 2 + core
@@ -219,22 +222,23 @@
             go(remote(slot, slot, ax_s.at[2], ax_r.at[src_x], r, xnext))
         go(remote(slot, slot, ap_s.at[hop], ap_r.at[src_x], r, mate))
 
-    for hop in (1, 2):
-        for way, step, to in ((0, -hop, zup), (1, hop, zdown)):
-            src_z, slot = z_arrived(step)
-            z_forward(slot, src_z, way, to, hop)
-            y_forward(slot, src_z)
-        if hop == 1:
-            y_relay(0)
-        else:
-            y_relay(-1)
-            y_relay(1)
-    z_up = (z + d + nz) % nz
-    src_z, slot = z_arrived(-3 * d)
-    z_forward(slot, src_z, 0, z_up * NY + y, 3)
+    for step in (-1, 1):
+        src_z, slot = z_arrived(step)
+        y_forward(slot, src_z)
+    y_relay(0)
+    z_far = ((z + 2 * d + nz) % nz) * NY + y
+    src_z, slot = z_arrived(-2 * d)
+    z_forward(slot, src_z, 0, z_far, 3)
+    z_forward(slot, src_z, 0, ((z + d + nz) % nz) * NY + y, 2)
     y_forward(slot, src_z)
-    src_z, slot = z_arrived(3 * d)
+    src_z, slot = z_arrived(2 * d)
+    z_forward(slot, src_z, 1, ((z - d + nz) % nz) * NY + y, 2)
     y_forward(slot, src_z)
+    y_relay(-1)
+    y_relay(1)
+    for step in (-3, 3):
+        src_z, slot = z_arrived(step)
+        y_forward(slot, src_z)
     x_arrived(-d, 1)
     y_relay(-2)
     y_relay(2)
@@ -304,12 +308,9 @@
     for k in range(KMAX):
         line = jnp.sum(colacc[k].T, axis=0, keepdims=True)
         own = own + jnp.where((which == listed[k]) & live[k], line, 0.0)
-    for q in range(NY):
-        colown[q] = own[:, q * 128 : (q + 1) * 128]
-    coly[y] = colown[y]
+    coly[y] = own
     for s in (2, 1, 3):
-        q = (y + s) % NY
-        go(remote(colown.at[q], coly.at[y], cy_s.at[s], cy_r.at[y], yrow(s), c))
+        go(remote(coly.at[y], coly.at[y], cy_s.at[s], cy_r.at[y], yrow(s), c))
     for s in range(1, n_col):
         far = (c + s) % n_col
         go(remote(rowpart.at[far], rowrecv.at[c], rs_s.at[s], rs_r.at[c], r, far))
@@ -325,15 +326,9 @@
         src = (z + s) % nz
         slot = colz.at[src]
         remote(slot, slot, cz_s.at[s], cz_r.at[src], r, c).wait_recv()
-    logfull[y] = jnp.log(jnp.sum(colz[...], axis=0))
-    for s in (2, 1, 3):
-        mine = logfull.at[y]
-        go(remote(mine, mine, cl_s.at[s], cl_r.at[y], yrow(s), c))
-    for s in (1, 3, 2):
-        src = (y + s) % NY
-        slot = logfull.at[src]
-        remote(slot, slot, cl_s.at[s], cl_r.at[src], r, c).wait_recv()
-    logs = jnp.concatenate([logfull[q] for q in range(NY)], axis=1)
+    logs = jnp.log(jnp.sum(colz[...], axis=0))
+    for q in range(NY):
+        logfull[q] = logs[:, q * 128 : (q + 1) * 128]
     per = 128 // STRIP
     lchunk[...] = logfull[r // per]
     lrecv[c] = lchunk[...]
@@ -417,9 +412,8 @@
         pltpu.VMEM((KMAX, n_b, desc), BF16),
         pltpu.VMEM((KMAX, n_col, n_b, n_a), F32),
         pltpu.VMEM((KMAX, n_b, 128), F32),
-        pltpu.VMEM((NY, n_col, 128), F32),
-        pltpu.VMEM((NY, n_col, 128), F32),
-        pltpu.VMEM((nz, n_col, 128), F32),
+        pltpu.VMEM((NY, n_col, n_b), F32),
+        pltpu.VMEM((nz, n_col, n_b), F32),
         pltpu.VMEM((n_col, 128), F32),
         pltpu.VMEM((n_col, n_col, 128), F32),
         pltpu.VMEM((NY, n_col, 128), F32),
@@ -437,7 +431,6 @@
         ((n_col,), (n_col,)),
         ((n_col,), (n_col,)),
         ((n_col,), (n_col,)),
-        ((NY,), (NY,)),
     ):
         scratch += [dma(sent), dma(received)]
     scratch.append(dma((6,)))

time: 62.3 us -> 57.6 us (0.925)
  Pallas kernels: 59 us -> 54.3 us
    pallas_call x1, Pallas kernels: 59 us -> 54.3 us  [local(): run(feat_a, feat_b.reshape(width // STRIP, STRIP, ch), conv_weight.reshap...]
where the time goes in v4:
time: 57.6 us; the launch traced here: 57.4 us
  Pallas kernels  54.3 us (94%)
  local copies, waits for them, and re-layouts  2.45 us (4%)
  between operations  0.64 us (1%)
    pallas_call x1, Pallas kernels, local(): run(feat_a, feat_b.reshape(width // STRIP, STRIP, ch), conv_weight.reshap...  54.3 us
    slice x2, local copies, waits for them, and re-layouts, local(): return (both[0:4], both[4:5])  2.45 us

profile of v4, /device:TPU:1, one launch (start us, length us, event | category | flops | bytes accessed | tf_op | source)
XLA Modules:
  0.0 57.4 jit_solution(17001932143621652010)
XLA Ops:
  0.6 54.3 %shard_map.77 = f32[8,128]{1,0:T(8,128)} custom-call(bf16[4,128,128]{2,1,0:T(8,128)(2,1)} %feat_a_in.1, bf16[8,16,128]{2,1,0:T(8,128)(2,1)} %bitcast.5, bf16[3,384,256]{2,1,0:T(8,128)(2,1)} %bitcast.4, f32[1,256]{1,0:T(1,128)} %bitcast.6, s32[2,32]{1,0:T(2,128)} %bitcast.7, s32[32]{0:T(128)} %counts.1), custom_call_target="tpu_custom_call" | custom-call | tf_op jit(solution)/shard_map/pallas_call | solution.py:447
  54.9 1.2 %slice.7 = f32[1,128]{1,0:T(1,128)} slice(f32[8,128]{1,0:T(8,128)} %shard_map.77), slice={[4:5], [0:128]} | slice | bytes 1024 | tf_op jit(solution)/shard_map/slice | solution.py:455
  56.1 1.3 %slice.6 = f32[4,128]{1,0:T(4,128)} slice(f32[8,128]{1,0:T(8,128)} %shard_map.77), slice={[0:4], [0:128]} | slice | bytes 4096 | tf_op jit(solution)/shard_map/slice | solution.py:455

commit v5 on v4

--- a/solution.py
+++ b/solution.py
@@ -301,7 +301,7 @@
         rowpart[j] = jnp.concatenate(rows + rows, axis=0)
         return carry
 
-    lax.fori_loop(0, n_col, first, 0)
+    lax.fori_loop(0, n_col, first, 0, unroll=2)
 
     which = lax.broadcasted_iota(jnp.int32, (n_col, n_b), 0)
     own = jnp.zeros((n_col, n_b), F32)
@@ -343,7 +343,8 @@
     for k in range(KMAX):
         colacc[k] = lower[k]
 
-    def second(j, carry):
+    def second(turn, carry):
+        j = (c + 1 + turn) % n_col
         best = [jnp.full((1, 128), -jnp.inf, F32) for _ in range(groups)]
         for k in range(KMAX):
             for g in range(groups):
@@ -351,12 +352,18 @@
                 top_of = jnp.max(candidate, axis=0, keepdims=True)
                 best[g] = jnp.maximum(best[g], jnp.where(live[k], top_of, -jnp.inf))
         maxpart[j] = jnp.concatenate(best + best, axis=0)
+
+        @pl.when(turn < n_col - 1)
+        def _():
+            slot = turn + 1
+            remote(maxpart.at[j], maxrecv.at[c], mx_s.at[slot], mx_r.at[c], r, j).start()
+
         return carry
 
-    lax.fori_loop(0, n_col, second, 0)
+    lax.fori_loop(0, n_col, second, 0, unroll=2)
     for s in range(1, n_col):
         far = (c + s) % n_col
-        go(remote(maxpart.at[far], maxrecv.at[c], mx_s.at[s], mx_r.at[c], r, far))
+        sends.append(remote(maxpart.at[far], maxrecv.at[c], mx_s.at[s], mx_r.at[c], r, far))
     maxrecv[c] = maxpart[c]
 
     for s in range(1, n_col):

time: 57.6 us -> 55.3 us (0.960)
  Pallas kernels: 54.3 us -> 52 us
    pallas_call x1, Pallas kernels: 54.3 us -> 52 us  [local(): run(feat_a, feat_b.reshape(width // STRIP, STRIP, ch), conv_weight.reshap...]
where the time goes in v5:
time: 55.3 us; the launch traced here: 55.1 us
  Pallas kernels  52 us (94%)
  local copies, waits for them, and re-layouts  2.45 us (4%)
  between operations  0.64 us (1%)
    pallas_call x1, Pallas kernels, local(): run(feat_a, feat_b.reshape(width // STRIP, STRIP, ch), conv_weight.reshap...  52 us
    slice x2, local copies, waits for them, and re-layouts, local(): return (both[0:4], both[4:5])  2.45 us

profile of v5, /device:TPU:1, one launch (start us, length us, event | category | flops | bytes accessed | tf_op | source)
XLA Modules:
  0.0 55.1 jit_solution(11911470859895936321)
XLA Ops:
  0.6 52.0 %shard_map.77 = f32[8,128]{1,0:T(8,128)} custom-call(bf16[4,128,128]{2,1,0:T(8,128)(2,1)} %feat_a_in.1, bf16[8,16,128]{2,1,0:T(8,128)(2,1)} %bitcast.5, bf16[3,384,256]{2,1,0:T(8,128)(2,1)} %bitcast.4, f32[1,256]{1,0:T(1,128)} %bitcast.6, s32[2,32]{1,0:T(2,128)} %bitcast.7, s32[32]{0:T(128)} %counts.1), custom_call_target="tpu_custom_call" | custom-call | tf_op jit(solution)/shard_map/pallas_call | solution.py:454
  52.7 1.2 %slice.7 = f32[1,128]{1,0:T(1,128)} slice(f32[8,128]{1,0:T(8,128)} %shard_map.77), slice={[4:5], [0:128]} | slice | bytes 1024 | tf_op jit(solution)/shard_map/slice | solution.py:462
  53.9 1.3 %slice.6 = f32[4,128]{1,0:T(4,128)} slice(f32[8,128]{1,0:T(8,128)} %shard_map.77), slice={[0:4], [0:128]} | slice | bytes 4096 | tf_op jit(solution)/shard_map/slice | solution.py:462
